TPU v7x, 256 devices: a whole 4x4x8 slice. The times are simulated.
256 devices in a mesh: inst: 8 (over y_hi, x), space: 32 (over z, y_lo, core).
Axes of the slice: x: 4, y: 4 (y_hi: 2, y_lo: 2; y = y_hi * 2 + y_lo), z: 8, core: 2. Of those that a mesh axis runs over, the one named last changes fastest.
Arguments:
- psi_start: float32 [5, 8, 256, 1024], P(None, 'inst', 'space'), may hold values from -6 to 6
- density: float32 [8, 256, 1024], P('inst', 'space'), may hold values from 0.8 to 1.25
- velocity: float32 [3, 8, 256, 1024], P(None, 'inst', 'space'), may hold values from -0.6 to 0.6
- pressure: float32 [8, 256, 1024], P('inst', 'space'), may hold values from 0.5 to 1
- obs_pos: float32 [3, 512], P(None, 'space'), may hold values from -16 to 16, as said below
- obs_weight: float32 [2, 512], P(None, 'space'), may hold values from -0.6 to 0.6
- obs_harmonic: int32 [512], P('space'), may hold values from 1 to 3
- panel_pos: float32 [3, 65536], replicated, may hold values from -1 to 1
- panel_normal: float32 [3, 65536], P(None, 'space'), may hold values from -5 to 5
- panel_cell: int32 [65536], P('space'), may hold values from 0 to 8191
- plane_nbr: int32 [4, 1024], replicated, may hold values from 0 to 1023
Outputs:
- adjoint: float32 [5, 8, 256, 1024], P(None, 'inst', 'space')
Inputs may be any that keep to these rules, and one draw needn't show every extreme that they name: `obs_pos`: observers lie between 8 and 16 from the anchor, outside the panels' cube. panel_cell[q] is an index into the 8 x 1024 cells of the slot's owner, layer panel_cell[q] // 1024.
All inputs are finite; a program needn't handle non-finite values.
Results may differ from a plain program's by a relative error of at most 0.0001.
Values sent between devices are 32-bit elements; how exact they have to be, the bound alone decides.
A program may use at most 64 MiB of HBM per device.

v0:
```python
import math
import jax
import jax.numpy as jnp
from jax import lax
from jax.sharding import PartitionSpec as P

ITERS = 3
GAMMA = 1.4
KWAVE = 0.7
RADIUS = 10.0
TAU = 0.05
DISSIP = 0.25
OMEGA = 1.5
VISCO = 0.5


def padded_2(cells, sides, width):
    for axis, dim in sides:
        count = lax.axis_size(axis)
        head = lax.slice_in_dim(cells, 0, width, axis=dim)
        tail = lax.slice_in_dim(cells, cells.shape[dim] - width, cells.shape[dim], axis=dim)
        cells = jnp.concatenate(
            [
                lax.ppermute(tail, axis, [(i, (i + 1) % count) for i in range(count)]),
                cells,
                lax.ppermute(head, axis, [((i + 1) % count, i) for i in range(count)]),
            ],
            axis=dim,
        )
    return cells


def panel_block(observers, panels, time_now):
    delta = panels[:, None, :] - observers[:3, :, None]
    dist2 = jnp.sum(delta * delta, axis=0)
    dist = jnp.sqrt(dist2)
    harm = observers[5][:, None]
    phase = harm * (time_now - KWAVE * dist)
    amp = (
        (observers[3][:, None] * jnp.cos(phase) + observers[4][:, None] * jnp.sin(phase))
        * (RADIUS * RADIUS)
        / (dist2 * dist)
    )
    return jnp.sum(amp[None] * delta, axis=1)


def sensitivity(observers, panels, time_now):
    count = panels.shape[1]
    obs_count = observers.shape[1]
    block = math.gcd(count, max(128, 262144 // obs_count))
    split = panels.reshape(3, count // block, block).transpose(1, 0, 2)
    out = lax.map(lambda piece: panel_block(observers, piece, time_now), split)
    return out.transpose(1, 0, 2).reshape(3, count)


def conserved(density, velocity, pressure):
    moment = density[None] * velocity
    energy = pressure / (GAMMA - 1.0) + 0.5 * density * jnp.sum(velocity * velocity, axis=0)
    return jnp.concatenate([density[None], moment, energy[None]], axis=0)


def fluxes(state):
    dens = state[0]
    moment = state[1:4]
    energy = state[4]
    vel = moment / dens
    press = (GAMMA - 1.0) * (energy - 0.5 * jnp.sum(moment * vel, axis=0))
    result = []
    for axis_d in range(3):
        comps = [moment[axis_d]]
        for axis_e in range(3):
            term = moment[axis_e] * vel[axis_d]
            if axis_e == axis_d:
                term = term + press
            comps.append(term)
        comps.append((energy + press) * vel[axis_d])
        result.append(jnp.stack(comps))
    return tuple(result)


def spectral_coeff(offset, count):
    safe = jnp.where(offset == 0, 1.0, offset)
    angle = math.pi * safe / count
    even_odd_flag = 1.0 - 2.0 * jnp.mod(safe, 2.0)
    other = (
        -(OMEGA / 2.0) * even_odd_flag * jnp.cos(angle) / jnp.sin(angle)
        + VISCO * (OMEGA * OMEGA / 2.0) * even_odd_flag / jnp.sin(angle) ** 2
    )
    return jnp.where(offset == 0, VISCO * OMEGA * OMEGA * (count * count + 2.0) / 12.0, other)


def shards(
    psi_start,
    density,
    velocity,
    pressure,
    obs_pos,
    obs_weight,
    obs_harmonic,
    panel_pos,
    panel_normal,
    panel_cell,
    plane_nbr,
):
    inst_count = lax.axis_size("inst")
    inst_id = lax.axis_index("inst")
    space_id = lax.axis_index("space")
    time_now = 2.0 * math.pi * inst_id.astype(jnp.float32) / inst_count
    observers = jnp.concatenate(
        [obs_pos, obs_weight, obs_harmonic[None].astype(jnp.float32)], axis=0
    )
    owned_count = panel_normal.shape[1]
    whole = sensitivity(observers, panel_pos, time_now)
    total = lax.psum(whole, "space")
    sens = lax.dynamic_slice_in_dim(total, space_id * owned_count, owned_count, 1)
    weight = jnp.sum(sens * panel_normal, axis=0)
    layers = psi_start.shape[2]
    plane = psi_start.shape[3]
    wall = jax.ops.segment_sum(weight, panel_cell, num_segments=layers * plane).reshape(
        layers, plane
    )
    dens = density[0]
    vel = velocity[:, 0]
    state = conserved(dens, vel, pressure[0])
    slope = jnp.concatenate(
        [0.5 * jnp.sum(vel * vel, axis=0)[None], -vel, jnp.ones_like(dens)[None]], axis=0
    ) * (GAMMA - 1.0)
    source = slope * wall[None]
    _, pull = jax.vjp(fluxes, state)
    psi = psi_start[:, 0]
    for step in range(ITERS):
        padded = padded_2(psi, (("space", 1),), 1)
        minus_a = padded[:, :-2]
        plus_a = padded[:, 2:]
        plus_y = jnp.take(psi, plane_nbr[0], axis=2)
        minus_y = jnp.take(psi, plane_nbr[1], axis=2)
        plus_z = jnp.take(psi, plane_nbr[2], axis=2)
        minus_z = jnp.take(psi, plane_nbr[3], axis=2)
        middle_point = pull(
            (0.5 * (minus_a - plus_a), 0.5 * (minus_y - plus_y), 0.5 * (minus_z - plus_z))
        )[0]
        spread = 6.0 * psi - (minus_a + plus_a + plus_y + minus_y + plus_z + minus_z)
        every_instant = lax.all_gather(psi[:, None], "inst", axis=1, tiled=True)
        others = jnp.arange(inst_count, dtype=jnp.int32)
        row_entry = spectral_coeff(
            jnp.mod(inst_id - others, inst_count).astype(jnp.float32), float(inst_count)
        )
        spectral_operator = jnp.einsum(
            "c,kcyo->kyo", row_entry, every_instant, precision=lax.Precision.HIGHEST
        )
        psi = psi - TAU * (middle_point + DISSIP * spread + spectral_operator + source)
    return psi[:, None]


def solution(mesh):
    placed = (
        P(None, "inst", "space", None),
        P("inst", "space", None),
        P(None, "inst", "space", None),
        P("inst", "space", None),
        P(None, "space"),
        P(None, "space"),
        P("space"),
        P(),
        P(None, "space"),
        P("space"),
        P(),
    )
    return jax.shard_map(
        shards,
        mesh=mesh,
        in_specs=placed,
        out_specs=P(None, "inst", "space", None),
        check_vma=False,
    )
```

profile of v0, /device:TPU:2, one launch (start us, length us, event | category | flops | bytes accessed | tf_op | source)
XLA Modules:
  0.0 505.2 jit_solution(14409982304165432410)
XLA Ops:
  8.0 38.1 %while.10 = (s32[]{:T(128)}, f32[4,3,16384]{2,1,0:T(4,128)}, f32[2,16]{1,0:T(2,128)}, f32[1,16]{1,0:T(1,128)S(1)}, f32[]{:T(128)}, /*index=5*/f32[4,3,16384]{2,1,0:T(4,128)}, f32[3,16]{1,0:T(4,128)}, s32[]{:T(128)}) while((s32[]{:T(128)}, f32[4,3,16384]{2,1,0:T(4,128)}, f32[2,16]{1,0:T(2,128)}, f32[1,16]{1,0:T(1,128)S(1)}, f32[]{:T(128)}, ...), condition=%wide.region_6.8_spmd, body=%wide.region_3.7_spmd.sunk | while | flops 6766594 | bytes 5637533 | solution.py:52
  11.1 4.3 fusion.108
  20.6 4.3 fusion.108
  30.1 4.3 fusion.108
  39.6 4.3 fusion.108
  47.3 6.4 %collective-permute-start.1 = (f32[5,1,1024]{2,1,0:T(1,128)S(1)}, f32[5,1,1024]{2,1,0:T(1,128)S(1)}, u32[]{:S(2)}, u32[]{:S(2)}) collective-permute-start(f32[5,1,1024]{2,1,0:T(1,128)S(1)} %get-tuple-element.159), channel_id=1, source_target_pairs={{1,0},{2,1},{3,2},{4,3},{5,4},{6,5},{7,6},{8,7},{9,8},{10,9},{11,1... | collective-permute-start | bytes 61448 | tf_op jit(solution)/shard_map/ppermute | solution.py:26
  56.5 10.4 %gather_fusion = f32[1024,5,8]{2,1,0:T(8,128)} fusion(f32[5,8,1024]{1,0,2:T(8,128)} %copy.184, s32[1024]{0:T(1024)S(1)} %fusion.60), kind=kCustom, calls=%fused_computation.clone | custom fusion | bytes 331776 | tf_op jit(solution)/shard_map/jit(_take)/gather | solution.py:138
  66.9 2.7 copy.185
  69.6 10.4 %gather_fusion.1 = f32[1024,5,8]{2,1,0:T(8,128)} fusion(f32[5,8,1024]{1,0,2:T(8,128)} %copy.184, s32[1024]{0:T(1024)S(1)} %fusion.61), kind=kCustom, calls=%fused_computation.1.clone | custom fusion | bytes 331776 | tf_op jit(solution)/shard_map/jit(_take)/gather | solution.py:137
  82.5 10.4 %gather_fusion.2 = f32[1024,5,8]{2,1,0:T(8,128)} fusion(f32[5,8,1024]{1,0,2:T(8,128)} %copy.184, s32[1024]{0:T(1024)S(1)} %fusion.62), kind=kCustom, calls=%fused_computation.2.clone | custom fusion | bytes 331776 | tf_op jit(solution)/shard_map/jit(_take)/gather | solution.py:136
  92.9 2.6 copy.189
  95.6 10.4 %gather_fusion.3 = f32[1024,5,8]{2,1,0:T(8,128)} fusion(f32[5,8,1024]{1,0,2:T(8,128)} %copy.184, s32[1024]{0:T(1024)S(1)} %fusion.63), kind=kCustom, calls=%fused_computation.3.clone | custom fusion | bytes 331776 | tf_op jit(solution)/shard_map/jit(_take)/gather | solution.py:135
  109.2 169.2 %all-reduce.80.cloned.1.call-done = f32[3,65536]{1,0:T(4,128)} async-done(((f32[3,65536]{1,0:T(4,128)}), f32[3,65536]{1,0:T(4,128)}) %all-reduce.80.cloned.1.call-update) | async-done | bytes 786448 | tf_op jit(solution)/shard_map/psum | solution.py:114
  279.1 11.6 %scatter_custom_fusion = f32[8192]{0:T(1024)S(1)} fusion(s32[2048]{0:T(1024)} %param.24, f32[2048]{0:T(1024)S(1)} %multiply_reduce_fusion.4, f32[]{:T(128)} %constant.59.clone.1), kind=kCustom, calls=%fused_computation.205 | custom fusion | flops 2048 | bytes 33280 | tf_op jit(solution)/shard_map/scatter-add | solution.py:119
  290.8 3.2 fusion.9
  294.2 2.7 copy.192
  296.8 10.4 %gather_fusion.4 = f32[1024,5,8]{2,1,0:T(8,128)} fusion(f32[5,8,1024]{1,0,2:T(8,128)} %copy.192, s32[1024]{0:T(1024)S(1)} %fusion.60), kind=kCustom, calls=%fused_computation.4.clone | custom fusion | bytes 331776 | tf_op jit(solution)/shard_map/jit(_take)/gather | solution.py:138
  307.2 10.3 %gather_fusion.5 = f32[1024,5,8]{2,1,0:T(8,128)} fusion(f32[5,8,1024]{1,0,2:T(8,128)} %copy.192, s32[1024]{0:T(1024)S(1)} %fusion.61), kind=kCustom, calls=%fused_computation.5.clone | custom fusion | bytes 331776 | tf_op jit(solution)/shard_map/jit(_take)/gather | solution.py:137
  317.5 10.4 %gather_fusion.6 = f32[1024,5,8]{2,1,0:T(8,128)} fusion(f32[5,8,1024]{1,0,2:T(8,128)} %copy.192, s32[1024]{0:T(1024)S(1)} %fusion.62), kind=kCustom, calls=%fused_computation.6.clone | custom fusion | bytes 331776 | tf_op jit(solution)/shard_map/jit(_take)/gather | solution.py:136
  327.9 10.4 %gather_fusion.7 = f32[1024,5,8]{2,1,0:T(8,128)} fusion(f32[5,8,1024]{1,0,2:T(8,128)} %copy.192, s32[1024]{0:T(1024)S(1)} %fusion.63), kind=kCustom, calls=%fused_computation.7.clone | custom fusion | bytes 331776 | tf_op jit(solution)/shard_map/jit(_take)/gather | solution.py:135
  343.5 2.6 copy.197
  349.1 4.1 collective-permute-start.3
  355.0 37.8 %all-gather.8.cloned.1.call-done = f32[5,64,1024]{2,1,0:T(8,128)} async-done(((f32[5,8,1024]{2,1,0:T(8,128)}), f32[5,64,1024]{2,1,0:T(8,128)}) %all-gather.8.cloned.1.call-update) | async-done | bytes 1310736 | tf_op jit(solution)/shard_map/all_gather | solution.py:143
  392.8 3.2 fusion.7
  396.2 2.7 copy.200
  398.8 10.4 %gather_fusion.8 = f32[1024,5,8]{2,1,0:T(8,128)} fusion(f32[5,8,1024]{1,0,2:T(8,128)} %copy.200, s32[1024]{0:T(1024)S(1)} %fusion.60), kind=kCustom, calls=%fused_computation.8.clone | custom fusion | bytes 331776 | tf_op jit(solution)/shard_map/jit(_take)/gather | solution.py:138
  409.2 10.3 %gather_fusion.9 = f32[1024,5,8]{2,1,0:T(8,128)} fusion(f32[5,8,1024]{1,0,2:T(8,128)} %copy.200, s32[1024]{0:T(1024)S(1)} %fusion.61), kind=kCustom, calls=%fused_computation.9.clone | custom fusion | bytes 331776 | tf_op jit(solution)/shard_map/jit(_take)/gather | solution.py:137
  419.5 10.4 %gather_fusion.10 = f32[1024,5,8]{2,1,0:T(8,128)} fusion(f32[5,8,1024]{1,0,2:T(8,128)} %copy.200, s32[1024]{0:T(1024)S(1)} %fusion.62), kind=kCustom, calls=%fused_computation.10.clone | custom fusion | bytes 331776 | tf_op jit(solution)/shard_map/jit(_take)/gather | solution.py:136
  429.9 10.4 %gather_fusion.11 = f32[1024,5,8]{2,1,0:T(8,128)} fusion(f32[5,8,1024]{1,0,2:T(8,128)} %copy.200, s32[1024]{0:T(1024)S(1)} %fusion.63), kind=kCustom, calls=%fused_computation.11.clone | custom fusion | bytes 331776 | tf_op jit(solution)/shard_map/jit(_take)/gather | solution.py:135
  451.1 3.8 collective-permute-start.5
  456.8 36.8 %all-gather.10.cloned.1.call-done = f32[5,64,1024]{2,1,0:T(8,128)} async-done(((f32[5,8,1024]{2,1,0:T(8,128)}), f32[5,64,1024]{2,1,0:T(8,128)}) %all-gather.10.cloned.1.call-update) | async-done | bytes 1310736 | tf_op jit(solution)/shard_map/all_gather | solution.py:143
  493.6 3.2 fusion.5
  (121 shorter events, 55.6 us)
Async XLA Ops:
  7.4 270.9 %all-reduce.80.cloned.1.call-start = ((), (), s32[]{:S(2)}) async-start(), calls=%async_computation.1 | async-start | bytes 2097152 | tf_op jit(solution)/shard_map/psum | solution.py:114
  8.0 45.8 %copy-start.4 = (f32[5,1,8,1024]{3,2,1,0:T(8,128)S(1)}, f32[5,1,8,1024]{3,2,1,0:T(8,128)}, u32[]{:S(2)}) copy-start(f32[5,1,8,1024]{3,2,1,0:T(8,128)} %param.15) | copy-start | bytes 491524
  46.1 10.3 %copy-start.9 = (s32[4,1024]{1,0:T(4,128)S(1)}, s32[4,1024]{1,0:T(4,128)}, u32[]{:S(2)}) copy-start(s32[4,1024]{1,0:T(4,128)} %param.25) | copy-start | bytes 49156
  46.2 244.6 %all-gather.6.cloned.1.call-start = ((), (), s32[]{:S(2)}) async-start(), calls=%async_computation | async-start | bytes 1474560 | tf_op jit(solution)/shard_map/all_gather | solution.py:143
  47.3 61.6 %collective-permute-start = (f32[5,1,1024]{2,1,0:T(1,128)S(1)}, f32[5,1,1024]{2,1,0:T(1,128)S(1)}, u32[]{:S(2)}, u32[]{:S(2)}) collective-permute-start(f32[5,1,1024]{2,1,0:T(1,128)S(1)} %get-tuple-element.160), channel_id=1, source_target_pairs={{0,1},{1,2},{2,3},{3,4},{4,5},{5,6},{6,7},{7,8},{8,9},{9,10},{10,1... | collective-permute-start | bytes 61448 | tf_op jit(solution)/shard_map/ppermute | solution.py:24
  47.3 61.5 %collective-permute-start.1 = (f32[5,1,1024]{2,1,0:T(1,128)S(1)}, f32[5,1,1024]{2,1,0:T(1,128)S(1)}, u32[]{:S(2)}, u32[]{:S(2)}) collective-permute-start(f32[5,1,1024]{2,1,0:T(1,128)S(1)} %get-tuple-element.159), channel_id=1, source_target_pairs={{1,0},{2,1},{3,2},{4,3},{5,4},{6,5},{7,6},{8,7},{9,8},{10,9},{11,1... | collective-permute-start | bytes 61448 | tf_op jit(solution)/shard_map/ppermute | solution.py:26
  53.8 339.0 %all-gather.8.cloned.1.call-start = ((), (), s32[]{:S(2)}) async-start(), calls=%async_computation.2 | async-start | bytes 1474560 | tf_op jit(solution)/shard_map/all_gather | solution.py:143
  92.9 15.7 %copy-start.5 = (f32[1,8,1024]{2,1,0:T(8,128)S(1)}, f32[1,8,1024]{2,1,0:T(8,128)}, u32[]{:S(2)}) copy-start(f32[1,8,1024]{2,1,0:T(8,128)} %param.16) | copy-start | bytes 98308
  92.9 15.7 %copy-start.6 = (f32[3,1,8,1024]{3,2,1,0:T(8,128)S(1)}, f32[3,1,8,1024]{3,2,1,0:T(8,128)}, u32[]{:S(2)}) copy-start(f32[3,1,8,1024]{3,2,1,0:T(8,128)} %param.17) | copy-start | bytes 294916
  92.9 15.8 %copy-start.7 = (f32[1,8,1024]{2,1,0:T(8,128)S(1)}, f32[1,8,1024]{2,1,0:T(8,128)}, u32[]{:S(2)}) copy-start(f32[1,8,1024]{2,1,0:T(8,128)} %param.18) | copy-start | bytes 98308
  106.0 3.0 copy-start.10
  106.0 172.4 %copy-start.8 = (f32[3,2048]{1,0:T(4,128)S(1)}, f32[3,2048]{1,0:T(4,128)}, u32[]{:S(2)}) copy-start(f32[3,2048]{1,0:T(4,128)} %param.23) | copy-start | bytes 73732
  294.1 44.1 %copy-start.2 = (f32[5,8,1024]{2,1,0:T(8,128)}, f32[5,8,1024]{2,1,0:T(8,128)S(1)}, u32[]{:S(2)}) copy-start(f32[5,8,1024]{2,1,0:T(8,128)S(1)} %fusion.36) | copy-start | bytes 491524
  338.3 155.3 %all-gather.10.cloned.1.call-start = ((), (), s32[]{:S(2)}) async-start(), calls=%async_computation.3 | async-start | bytes 1474560 | tf_op jit(solution)/shard_map/all_gather | solution.py:143
  343.5 5.2 %copy-start.3 = (f32[5,8,1024]{2,1,0:T(8,128)S(1)}, f32[5,8,1024]{2,1,0:T(8,128)}, u32[]{:S(2)}) copy-start(f32[5,8,1024]{2,1,0:T(8,128)} %copy-done.2) | copy-start | bytes 491524
  348.8 5.8 %collective-permute-start.2 = (f32[5,1,1024]{2,1,0:T(1,128)S(1)}, f32[5,1,1024]{2,1,0:T(1,128)S(1)}, u32[]{:S(2)}, u32[]{:S(2)}) collective-permute-start(f32[5,1,1024]{2,1,0:T(1,128)S(1)} %get-tuple-element.148), channel_id=1, source_target_pairs={{0,1},{1,2},{2,3},{3,4},{4,5},{5,6},{6,7},{7,8},{8,9},{9,10},{10,1... | collective-permute-start | bytes 61448 | tf_op jit(solution)/shard_map/ppermute | solution.py:24
  349.1 5.6 %collective-permute-start.3 = (f32[5,1,1024]{2,1,0:T(1,128)S(1)}, f32[5,1,1024]{2,1,0:T(1,128)S(1)}, u32[]{:S(2)}, u32[]{:S(2)}) collective-permute-start(f32[5,1,1024]{2,1,0:T(1,128)S(1)} %get-tuple-element.147), channel_id=1, source_target_pairs={{1,0},{2,1},{3,2},{4,3},{5,4},{6,5},{7,6},{8,7},{9,8},{10,9},{11,1... | collective-permute-start | bytes 61448 | tf_op jit(solution)/shard_map/ppermute | solution.py:26
  396.2 44.1 %copy-start = (f32[5,8,1024]{2,1,0:T(8,128)}, f32[5,8,1024]{2,1,0:T(8,128)S(1)}, u32[]{:S(2)}) copy-start(f32[5,8,1024]{2,1,0:T(8,128)S(1)} %fusion.25) | copy-start | bytes 491524
  445.5 5.2 %copy-start.1 = (f32[5,8,1024]{2,1,0:T(8,128)S(1)}, f32[5,8,1024]{2,1,0:T(8,128)}, u32[]{:S(2)}) copy-start(f32[5,8,1024]{2,1,0:T(8,128)} %copy-done) | copy-start | bytes 491524
  450.8 5.7 %collective-permute-start.4 = (f32[5,1,1024]{2,1,0:T(1,128)S(1)}, f32[5,1,1024]{2,1,0:T(1,128)S(1)}, u32[]{:S(2)}, u32[]{:S(2)}) collective-permute-start(f32[5,1,1024]{2,1,0:T(1,128)S(1)} %get-tuple-element.137), channel_id=1, source_target_pairs={{0,1},{1,2},{2,3},{3,4},{4,5},{5,6},{6,7},{7,8},{8,9},{9,10},{10,1... | collective-permute-start | bytes 61448 | tf_op jit(solution)/shard_map/ppermute | solution.py:24
  451.1 5.4 %collective-permute-start.5 = (f32[5,1,1024]{2,1,0:T(1,128)S(1)}, f32[5,1,1024]{2,1,0:T(1,128)S(1)}, u32[]{:S(2)}, u32[]{:S(2)}) collective-permute-start(f32[5,1,1024]{2,1,0:T(1,128)S(1)} %get-tuple-element.136), channel_id=1, source_target_pairs={{1,0},{2,1},{3,2},{4,3},{5,4},{6,5},{7,6},{8,7},{9,8},{10,9},{11,1... | collective-permute-start | bytes 61448 | tf_op jit(solution)/shard_map/ppermute | solution.py:26
Sparse Core Ops, SparseCore 0:
  46.3 231.9 all-reduce.79
Sparse Core Ops, SparseCore 1:
  53.8 54.9 all-gather.5
  338.4 54.4 all-gather.7
  440.4 53.2 all-gather.9
where the time goes:
time: 506 us; the launch traced here: 505 us
  waiting for transfers between devices  247 us (49%)
  local copies, waits for them, and re-layouts  175 us (35%)
  other arithmetic  43.5 us (9%)
  between operations  15.5 us (3%)
  starting transfers between devices  15.1 us (3%)
  matrix products  9.46 us (2%)
    psum x1, waiting for transfers between devices, shards(): total = lax.psum(whole, 'space')  169 us
    all_gather x3, waiting for transfers between devices, shards(): every_instant = lax.all_gather(psi[:, None], 'inst', axis=1, tiled=True)  74.7 us
    gather x6, local copies, waits for them, and re-layouts, shards(): minus_y = jnp.take(psi, plane_nbr[1], axis=2)  39.1 us
    gather x6, local copies, waits for them, and re-layouts, shards(): plus_y = jnp.take(psi, plane_nbr[0], axis=2)  39 us
    gather x6, local copies, waits for them, and re-layouts, shards(): minus_z = jnp.take(psi, plane_nbr[3], axis=2)  38.9 us
    gather x6, local copies, waits for them, and re-layouts, shards(): plus_z = jnp.take(psi, plane_nbr[2], axis=2)  38.8 us
    div x4, other arithmetic, panel_block(): (observers[3][:, None] * jnp.cos(phase) + observers[4][:, None] * jnp.sin...  17.3 us
    ppermute x3, starting transfers between devices, padded_2(): lax.ppermute(head, axis, [((i + 1) % count, i) for i in range(count)])  14.3 us
  transfers between devices with their start and end apart: 10, of which 5 were waited for; matrix products, arithmetic and copies ran while one was open for 18% of the time, Pallas kernels for 0%

commit v1 on v0

--- a/solution.py
+++ b/solution.py
@@ -111,7 +111,7 @@
     )
     owned_count = panel_normal.shape[1]
     whole = sensitivity(observers, panel_pos, time_now)
-    total = lax.psum(whole, "space")
+    total = jnp.sum(lax.all_gather(whole, "space"), axis=0)
     sens = lax.dynamic_slice_in_dim(total, space_id * owned_count, owned_count, 1)
     weight = jnp.sum(sens * panel_normal, axis=0)
     layers = psi_start.shape[2]

time: 506 us -> 412 us (0.81)
  waiting for transfers between devices: 247 us -> 141 us
  other arithmetic: 43.5 us -> 55.5 us
    psum x1 -> x0, waiting for transfers between devices: 169 us -> none  [shards(): total = lax.psum(whole, 'space')]
    all_gather x0 -> x1, waiting for transfers between devices: none -> 140 us  [shards(): total = jnp.sum(lax.all_gather(whole, 'space'), axis=0)]
    all_gather x3, waiting for transfers between devices: 74.7 us -> 0.06 us  [shards(): every_instant = lax.all_gather(psi[:, None], 'inst', axis=1, tiled=True)]
    reduce_sum x0 -> x1, other arithmetic: none -> 11.5 us  [shards(): total = jnp.sum(lax.all_gather(whole, 'space'), axis=0)]
  transfers between devices with their start and end apart: 10 -> 10, of which waited for: 5 -> 1; matrix products, arithmetic and copies ran while one was open for 18% -> 51% of each run, Pallas kernels for 0% -> 0%
where the time goes in v1:
time: 412 us; the launch traced here: 411 us
  local copies, waits for them, and re-layouts  177 us (43%)
  waiting for transfers between devices  141 us (34%)
  other arithmetic  55.5 us (13%)
  starting transfers between devices  14.4 us (3%)
  between operations  13.6 us (3%)
  matrix products  9.5 us (2%)
    all_gather x1, waiting for transfers between devices, shards(): total = jnp.sum(lax.all_gather(whole, 'space'), axis=0)  140 us
    gather x6, local copies, waits for them, and re-layouts, shards(): minus_y = jnp.take(psi, plane_nbr[1], axis=2)  39.5 us
    gather x6, local copies, waits for them, and re-layouts, shards(): minus_z = jnp.take(psi, plane_nbr[3], axis=2)  39.3 us
    gather x6, local copies, waits for them, and re-layouts, shards(): plus_y = jnp.take(psi, plane_nbr[0], axis=2)  39 us
    gather x6, local copies, waits for them, and re-layouts, shards(): plus_z = jnp.take(psi, plane_nbr[2], axis=2)  39 us
    div x4, other arithmetic, panel_block(): (observers[3][:, None] * jnp.cos(phase) + observers[4][:, None] * jnp.sin...  17.4 us
    ppermute x3, starting transfers between devices, padded_2(): lax.ppermute(head, axis, [((i + 1) % count, i) for i in range(count)])  14.3 us
    reduce_sum x1, other arithmetic, shards(): total = jnp.sum(lax.all_gather(whole, 'space'), axis=0)  11.5 us
  transfers between devices with their start and end apart: 10, of which 1 were waited for; matrix products, arithmetic and copies ran while one was open for 51% of the time, Pallas kernels for 0%

profile of v1, /device:TPU:2, one launch (start us, length us, event | category | flops | bytes accessed | tf_op | source)
XLA Modules:
  0.0 411.0 jit_solution(11977329365380571743)
XLA Ops:
  8.0 38.2 %while.10 = (s32[]{:T(128)}, f32[4,3,16384]{2,1,0:T(4,128)}, f32[2,16]{1,0:T(2,128)}, f32[1,16]{1,0:T(1,128)S(1)}, f32[]{:T(128)}, /*index=5*/f32[4,3,16384]{2,1,0:T(4,128)}, f32[3,16]{1,0:T(4,128)}, s32[]{:T(128)}) while((s32[]{:T(128)}, f32[4,3,16384]{2,1,0:T(4,128)}, f32[2,16]{1,0:T(2,128)}, f32[1,16]{1,0:T(1,128)S(1)}, f32[]{:T(128)}, ...), condition=%wide.region_6.8_spmd, body=%wide.region_3.7_spmd.sunk | while | flops 6766594 | bytes 5637033 | solution.py:52
  11.0 4.3 %fusion.108 = f32[16,16384]{1,0:T(8,128)S(1)} fusion(f32[16,16384]{1,0:T(8,128)S(1)} %fusion.107, f32[16]{0:T(128)S(1)} %get-tuple-element.238, f32[]{:T(128)} %get-tuple-element.260, f32[16]{0:T(128)S(1)} %bitcast.221, f32[16]{0:T(128)S(1)} %get-tuple-element.239), kind=kLoop, calls=%fused_computation.21.clone.1 | loop fusion | flops 2359296 | bytes 2097348 | tf_op jit(solution)/shard_map/while/body/eval_jaxpr/div | solution.py:40
  20.5 4.3 %fusion.108 = f32[16,16384]{1,0:T(8,128)S(1)} fusion(f32[16,16384]{1,0:T(8,128)S(1)} %fusion.107, f32[16]{0:T(128)S(1)} %get-tuple-element.238, f32[]{:T(128)} %get-tuple-element.260, f32[16]{0:T(128)S(1)} %bitcast.221, f32[16]{0:T(128)S(1)} %get-tuple-element.239), kind=kLoop, calls=%fused_computation.21.clone.1 | loop fusion | flops 2359296 | bytes 2097348 | tf_op jit(solution)/shard_map/while/body/eval_jaxpr/div | solution.py:40
  30.0 4.3 %fusion.108 = f32[16,16384]{1,0:T(8,128)S(1)} fusion(f32[16,16384]{1,0:T(8,128)S(1)} %fusion.107, f32[16]{0:T(128)S(1)} %get-tuple-element.238, f32[]{:T(128)} %get-tuple-element.260, f32[16]{0:T(128)S(1)} %bitcast.221, f32[16]{0:T(128)S(1)} %get-tuple-element.239), kind=kLoop, calls=%fused_computation.21.clone.1 | loop fusion | flops 2359296 | bytes 2097348 | tf_op jit(solution)/shard_map/while/body/eval_jaxpr/div | solution.py:40
  39.6 4.3 %fusion.108 = f32[16,16384]{1,0:T(8,128)S(1)} fusion(f32[16,16384]{1,0:T(8,128)S(1)} %fusion.107, f32[16]{0:T(128)S(1)} %get-tuple-element.238, f32[]{:T(128)} %get-tuple-element.260, f32[16]{0:T(128)S(1)} %bitcast.221, f32[16]{0:T(128)S(1)} %get-tuple-element.239), kind=kLoop, calls=%fused_computation.21.clone.1 | loop fusion | flops 2359296 | bytes 2097348 | tf_op jit(solution)/shard_map/while/body/eval_jaxpr/div | solution.py:40
  46.3 6.4 %collective-permute-start.1 = (f32[5,1,1024]{2,1,0:T(1,128)S(1)}, f32[5,1,1024]{2,1,0:T(1,128)S(1)}, u32[]{:S(2)}, u32[]{:S(2)}) collective-permute-start(f32[5,1,1024]{2,1,0:T(1,128)S(1)} %get-tuple-element.159), channel_id=1, source_target_pairs={{1,0},{2,1},{3,2},{4,3},{5,4},{6,5},{7,6},{8,7},{9,8},{10,9},{11,1... | collective-permute-start | bytes 61448 | tf_op jit(solution)/shard_map/ppermute | solution.py:26
  52.7 2.7 copy.184
  55.4 10.4 %gather_fusion.3 = f32[1024,5,8]{2,1,0:T(8,128)} fusion(f32[5,8,1024]{1,0,2:T(8,128)} %copy.184, s32[1024]{0:T(1024)S(1)} %fusion.63), kind=kCustom, calls=%fused_computation.3.clone | custom fusion | bytes 331776 | tf_op jit(solution)/shard_map/jit(_take)/gather | solution.py:135
  68.4 10.4 %gather_fusion.2 = f32[1024,5,8]{2,1,0:T(8,128)} fusion(f32[5,8,1024]{1,0,2:T(8,128)} %copy.184, s32[1024]{0:T(1024)S(1)} %fusion.62), kind=kCustom, calls=%fused_computation.2.clone | custom fusion | bytes 331776 | tf_op jit(solution)/shard_map/jit(_take)/gather | solution.py:136
  78.8 3.3 copy.189
  82.0 10.4 %gather_fusion.1 = f32[1024,5,8]{2,1,0:T(8,128)} fusion(f32[5,8,1024]{1,0,2:T(8,128)} %copy.184, s32[1024]{0:T(1024)S(1)} %fusion.61), kind=kCustom, calls=%fused_computation.1.clone | custom fusion | bytes 331776 | tf_op jit(solution)/shard_map/jit(_take)/gather | solution.py:137
  92.4 2.6 copy.187
  95.1 10.4 %gather_fusion = f32[1024,5,8]{2,1,0:T(8,128)} fusion(f32[5,8,1024]{1,0,2:T(8,128)} %copy.184, s32[1024]{0:T(1024)S(1)} %fusion.60), kind=kCustom, calls=%fused_computation.clone | custom fusion | bytes 331776 | tf_op jit(solution)/shard_map/jit(_take)/gather | solution.py:138
  105.4 2.7 copy.185
  108.7 3.2 fusion.9
  111.9 140.4 %all-gather.9.cloned.1.call-done = f32[32,3,65536]{2,1,0:T(4,128)} async-done(((f32[1,3,65536]{2,1,0:T(4,128)}), f32[32,3,65536]{2,1,0:T(4,128)}) %all-gather.9.cloned.1.call-update) | async-done | bytes 25165840 | tf_op jit(solution)/shard_map/all_gather | solution.py:114
  252.3 11.5 %reduce_sum.92 = f32[3,65536]{1,0:T(4,128)S(1)} reduce(f32[32,3,65536]{2,1,0:T(4,128)} %all-gather.9.cloned.1.call-done, f32[]{:T(128)} %constant.59.clone.1), dimensions={0}, to_apply=%region_7.9 | reduce | flops 6094848 | bytes 25952260 | tf_op jit(solution)/shard_map/reduce_sum | solution.py:114
  263.8 11.4 %scatter_custom_fusion = f32[8192]{0:T(1024)S(1)} fusion(s32[2048]{0:T(1024)} %param.24, f32[2048]{0:T(1024)S(1)} %multiply_reduce_fusion.4, f32[]{:T(128)} %constant.59.clone.1), kind=kCustom, calls=%fused_computation.205 | custom fusion | flops 2048 | bytes 33280 | tf_op jit(solution)/shard_map/scatter-add | solution.py:119
  276.2 3.5 copy.192
  279.7 10.4 %gather_fusion.7 = f32[1024,5,8]{2,1,0:T(8,128)} fusion(f32[5,8,1024]{1,0,2:T(8,128)} %copy.192, s32[1024]{0:T(1024)S(1)} %fusion.63), kind=kCustom, calls=%fused_computation.7.clone | custom fusion | bytes 331776 | tf_op jit(solution)/shard_map/jit(_take)/gather | solution.py:135
  290.1 10.3 %gather_fusion.6 = f32[1024,5,8]{2,1,0:T(8,128)} fusion(f32[5,8,1024]{1,0,2:T(8,128)} %copy.192, s32[1024]{0:T(1024)S(1)} %fusion.62), kind=kCustom, calls=%fused_computation.6.clone | custom fusion | bytes 331776 | tf_op jit(solution)/shard_map/jit(_take)/gather | solution.py:136
  300.5 10.4 %gather_fusion.5 = f32[1024,5,8]{2,1,0:T(8,128)} fusion(f32[5,8,1024]{1,0,2:T(8,128)} %copy.192, s32[1024]{0:T(1024)S(1)} %fusion.61), kind=kCustom, calls=%fused_computation.5.clone | custom fusion | bytes 331776 | tf_op jit(solution)/shard_map/jit(_take)/gather | solution.py:137
  310.9 10.5 %gather_fusion.4 = f32[1024,5,8]{2,1,0:T(8,128)} fusion(f32[5,8,1024]{1,0,2:T(8,128)} %copy.192, s32[1024]{0:T(1024)S(1)} %fusion.60), kind=kCustom, calls=%fused_computation.4.clone | custom fusion | bytes 331776 | tf_op jit(solution)/shard_map/jit(_take)/gather | solution.py:138
  321.4 4.0 collective-permute-start.3
  336.3 3.2 fusion.7
  340.3 3.5 copy.200
  343.9 10.4 %gather_fusion.11 = f32[1024,5,8]{2,1,0:T(8,128)} fusion(f32[5,8,1024]{1,0,2:T(8,128)} %copy.200, s32[1024]{0:T(1024)S(1)} %fusion.63), kind=kCustom, calls=%fused_computation.11.clone | custom fusion | bytes 331776 | tf_op jit(solution)/shard_map/jit(_take)/gather | solution.py:135
  354.3 10.3 %gather_fusion.10 = f32[1024,5,8]{2,1,0:T(8,128)} fusion(f32[5,8,1024]{1,0,2:T(8,128)} %copy.200, s32[1024]{0:T(1024)S(1)} %fusion.62), kind=kCustom, calls=%fused_computation.10.clone | custom fusion | bytes 331776 | tf_op jit(solution)/shard_map/jit(_take)/gather | solution.py:136
  364.6 10.4 %gather_fusion.9 = f32[1024,5,8]{2,1,0:T(8,128)} fusion(f32[5,8,1024]{1,0,2:T(8,128)} %copy.200, s32[1024]{0:T(1024)S(1)} %fusion.61), kind=kCustom, calls=%fused_computation.9.clone | custom fusion | bytes 331776 | tf_op jit(solution)/shard_map/jit(_take)/gather | solution.py:137
  375.0 10.5 %gather_fusion.8 = f32[1024,5,8]{2,1,0:T(8,128)} fusion(f32[5,8,1024]{1,0,2:T(8,128)} %copy.200, s32[1024]{0:T(1024)S(1)} %fusion.60), kind=kCustom, calls=%fused_computation.8.clone | custom fusion | bytes 331776 | tf_op jit(solution)/shard_map/jit(_take)/gather | solution.py:138
  385.6 3.9 collective-permute-start.5
  400.4 3.2 fusion.5
  (118 shorter events, 49.7 us)
Async XLA Ops:
  6.5 102.2 %all-gather.7.cloned.1.call-start = ((), (), s32[]{:S(2)}) async-start(), calls=%async_computation | async-start | bytes 1474560 | tf_op jit(solution)/shard_map/all_gather | solution.py:143
  7.3 245.0 %all-gather.9.cloned.1.call-start = ((), (), s32[]{:S(2)}) async-start(), calls=%async_computation.1 | async-start | bytes 34603008 | tf_op jit(solution)/shard_map/all_gather | solution.py:114
  8.0 38.2 %copy-start.2 = (f32[5,1,8,1024]{3,2,1,0:T(8,128)S(1)}, f32[5,1,8,1024]{3,2,1,0:T(8,128)}, u32[]{:S(2)}) copy-start(f32[5,1,8,1024]{3,2,1,0:T(8,128)} %param.15) | copy-start | bytes 491524
  46.1 9.2 %copy-start.7 = (s32[4,1024]{1,0:T(4,128)S(1)}, s32[4,1024]{1,0:T(4,128)}, u32[]{:S(2)}) copy-start(s32[4,1024]{1,0:T(4,128)} %param.25) | copy-start | bytes 49156
  46.2 290.1 %all-gather.11.cloned.1.call-start = ((), (), s32[]{:S(2)}) async-start(), calls=%async_computation.2 | async-start | bytes 1474560 | tf_op jit(solution)/shard_map/all_gather | solution.py:143
  46.3 62.1 %collective-permute-start.1 = (f32[5,1,1024]{2,1,0:T(1,128)S(1)}, f32[5,1,1024]{2,1,0:T(1,128)S(1)}, u32[]{:S(2)}, u32[]{:S(2)}) collective-permute-start(f32[5,1,1024]{2,1,0:T(1,128)S(1)} %get-tuple-element.159), channel_id=1, source_target_pairs={{1,0},{2,1},{3,2},{4,3},{5,4},{6,5},{7,6},{8,7},{9,8},{10,9},{11,1... | collective-permute-start | bytes 61448 | tf_op jit(solution)/shard_map/ppermute | solution.py:26
  52.7 55.7 %collective-permute-start = (f32[5,1,1024]{2,1,0:T(1,128)S(1)}, f32[5,1,1024]{2,1,0:T(1,128)S(1)}, u32[]{:S(2)}, u32[]{:S(2)}) collective-permute-start(f32[5,1,1024]{2,1,0:T(1,128)S(1)} %get-tuple-element.160), channel_id=1, source_target_pairs={{0,1},{1,2},{2,3},{3,4},{4,5},{5,6},{6,7},{7,8},{8,9},{9,10},{10,1... | collective-permute-start | bytes 61448 | tf_op jit(solution)/shard_map/ppermute | solution.py:24
  92.4 15.7 %copy-start.3 = (f32[1,8,1024]{2,1,0:T(8,128)S(1)}, f32[1,8,1024]{2,1,0:T(8,128)}, u32[]{:S(2)}) copy-start(f32[1,8,1024]{2,1,0:T(8,128)} %param.16) | copy-start | bytes 98308
  92.4 15.7 %copy-start.4 = (f32[3,1,8,1024]{3,2,1,0:T(8,128)S(1)}, f32[3,1,8,1024]{3,2,1,0:T(8,128)}, u32[]{:S(2)}) copy-start(f32[3,1,8,1024]{3,2,1,0:T(8,128)} %param.17) | copy-start | bytes 294916
  92.4 15.8 %copy-start.5 = (f32[1,8,1024]{2,1,0:T(8,128)S(1)}, f32[1,8,1024]{2,1,0:T(8,128)}, u32[]{:S(2)}) copy-start(f32[1,8,1024]{2,1,0:T(8,128)} %param.18) | copy-start | bytes 98308
  105.4 3.1 copy-start.8
  111.9 151.8 %copy-start.6 = (f32[3,2048]{1,0:T(4,128)S(1)}, f32[3,2048]{1,0:T(4,128)}, u32[]{:S(2)}) copy-start(f32[3,2048]{1,0:T(4,128)} %param.23) | copy-start | bytes 73732
  276.1 45.2 %copy-start.1 = (f32[5,8,1024]{2,1,0:T(8,128)S(1)}, f32[5,8,1024]{2,1,0:T(8,128)}, u32[]{:S(2)}) copy-start(f32[5,8,1024]{2,1,0:T(8,128)} %fusion.36) | copy-start | bytes 491524
  276.2 124.2 %all-gather.13.cloned.1.call-start = ((), (), s32[]{:S(2)}) async-start(), calls=%async_computation.3 | async-start | bytes 1474560 | tf_op jit(solution)/shard_map/all_gather | solution.py:143
  321.4 14.5 %collective-permute-start.3 = (f32[5,1,1024]{2,1,0:T(1,128)S(1)}, f32[5,1,1024]{2,1,0:T(1,128)S(1)}, u32[]{:S(2)}, u32[]{:S(2)}) collective-permute-start(f32[5,1,1024]{2,1,0:T(1,128)S(1)} %get-tuple-element.147), channel_id=1, source_target_pairs={{1,0},{2,1},{3,2},{4,3},{5,4},{6,5},{7,6},{8,7},{9,8},{10,9},{11,1... | collective-permute-start | bytes 61448 | tf_op jit(solution)/shard_map/ppermute | solution.py:26
  325.4 10.5 %collective-permute-start.2 = (f32[5,1,1024]{2,1,0:T(1,128)S(1)}, f32[5,1,1024]{2,1,0:T(1,128)S(1)}, u32[]{:S(2)}, u32[]{:S(2)}) collective-permute-start(f32[5,1,1024]{2,1,0:T(1,128)S(1)} %get-tuple-element.148), channel_id=1, source_target_pairs={{0,1},{1,2},{2,3},{3,4},{4,5},{5,6},{6,7},{7,8},{8,9},{9,10},{10,1... | collective-permute-start | bytes 61448 | tf_op jit(solution)/shard_map/ppermute | solution.py:24
  340.3 45.2 %copy-start = (f32[5,8,1024]{2,1,0:T(8,128)S(1)}, f32[5,8,1024]{2,1,0:T(8,128)}, u32[]{:S(2)}) copy-start(f32[5,8,1024]{2,1,0:T(8,128)} %fusion.25) | copy-start | bytes 491524
  385.6 14.4 %collective-permute-start.5 = (f32[5,1,1024]{2,1,0:T(1,128)S(1)}, f32[5,1,1024]{2,1,0:T(1,128)S(1)}, u32[]{:S(2)}, u32[]{:S(2)}) collective-permute-start(f32[5,1,1024]{2,1,0:T(1,128)S(1)} %get-tuple-element.136), channel_id=1, source_target_pairs={{1,0},{2,1},{3,2},{4,3},{5,4},{6,5},{7,6},{8,7},{9,8},{10,9},{11,1... | collective-permute-start | bytes 61448 | tf_op jit(solution)/shard_map/ppermute | solution.py:26
  389.5 10.5 %collective-permute-start.4 = (f32[5,1,1024]{2,1,0:T(1,128)S(1)}, f32[5,1,1024]{2,1,0:T(1,128)S(1)}, u32[]{:S(2)}, u32[]{:S(2)}) collective-permute-start(f32[5,1,1024]{2,1,0:T(1,128)S(1)} %get-tuple-element.137), channel_id=1, source_target_pairs={{0,1},{1,2},{2,3},{3,4},{4,5},{5,6},{6,7},{7,8},{8,9},{9,10},{10,1... | collective-permute-start | bytes 61448 | tf_op jit(solution)/shard_map/ppermute | solution.py:24
Sparse Core Ops, SparseCore 0:
  10.0 57.2 all-gather.6
  69.1 183.1 all-gather.8
  276.3 54.1 all-gather.10
  340.5 53.2 all-gather.12
